TPU v7x, 32 devices: a whole 2x2x4 slice. The times are simulated.
32 devices in a mesh: front: 1, row: 16 (over z, y, x), col: 2 (over core).
Axes of the slice: x: 2, y: 2, z: 4, core: 2. Of those that a mesh axis runs over, the one named last changes fastest.
Arguments:
- contributions: float32 [16, 128, 4096], P(('front', 'row'), None, 'col'), may hold values from -0.176776695 to 0.176776695
- valid_rows: int32 [16], P(('front', 'row')), may hold values from 1 to 128, 1280 in all
Outputs:
- r_rows: float32 [512, 4096], P('front', 'col')
All inputs are finite; a program needn't handle non-finite values. No bound on the sum of `valid_rows` on one device may be relied on, other than what follows from the above.
Results may differ from a plain program's by a relative error of at most 0.0003.
Values sent between devices are 32-bit elements; how exact they have to be, the bound alone decides.
A program may use at most 64 MiB of HBM per device.

v0:
```python
import functools

import jax
import jax.numpy as jnp
from jax import lax
from jax.experimental import pallas as pl
from jax.experimental.pallas import tpu as pltpu
from jax.sharding import PartitionSpec as P

PANEL = 256
NPANEL = 2
LANES = 128
SUB = 8
HIGHEST = lax.Precision.HIGHEST
MESH = pl.DeviceIdType.MESH


def spread(block, axis, owner):
    block = jnp.where(lax.axis_index(axis) == owner, block, jnp.zeros_like(block))
    return lax.psum(block, axis)


def inner_cols(left, right):
    return jnp.einsum("rp,rc->pc", left, right, precision=HIGHEST)


def by_psum(frontal, leading):
    width_local = frontal.shape[1]
    leading_cols = spread(frontal[:, :leading], "col", 0)
    gram_total = lax.psum(inner_cols(leading_cols, leading_cols), "row")
    factor = jnp.linalg.cholesky(gram_total)
    identity = jnp.eye(leading, dtype=jnp.float32)
    inverse = jax.scipy.linalg.solve_triangular(factor, identity, lower=True)
    first_basis = jnp.dot(leading_cols, inverse.T, precision=HIGHEST)
    projected = lax.psum(inner_cols(first_basis, frontal), "row")
    column_ids = lax.axis_index("col") * width_local + jnp.arange(width_local, dtype=jnp.int32)
    kept_mask = column_ids[None, :] >= jnp.arange(leading, dtype=jnp.int32)[:, None]
    return jnp.where(kept_mask, projected, jnp.zeros_like(projected))


def dot_t(left, right):
    return lax.dot_general(
        left, right, (((0,), (0,)), ((), ())), precision=HIGHEST, preferred_element_type=jnp.float32
    )


def inverse_factor(read, hooks):
    groups = LANES // SUB
    tile = (SUB, LANES)
    row = lax.broadcasted_iota(jnp.int32, tile, 0)
    col = lax.broadcasted_iota(jnp.int32, tile, 1)
    a = [read(g) for g in range(groups)]
    b = [jnp.where(row + g * SUB == col, 1.0, 0.0).astype(jnp.float32) for g in range(groups)]

    def columns(value, home):
        first = home * SUB
        return [jnp.broadcast_to(value[:, first + t : first + t + 1], tile) for t in range(SUB)]

    def across(value, t):
        return jnp.broadcast_to(value[t : t + 1, :], tile)

    for home in range(groups):
        if home in hooks:
            hooks[home]()
        f = columns(a[home], home)
        arow, brow = a[home], b[home]
        scaled, factors = [], []
        diag = f[0]
        for t in range(SUB):
            pinv = 1.0 / across(f[t], t)
            diag = jnp.where(row == t, f[t], diag)
            srow = across(arow, t) * pinv
            trow = across(brow, t) * pinv
            later = [across(f[u], t) * pinv for u in range(t + 1, SUB)]
            below = jnp.where(row > t, f[t], 0.0)
            for u in range(t + 1, SUB):
                f[u] = f[u] - below * later[u - t - 1]
            if t < SUB - 1:
                arow = arow - below * srow
                brow = brow - below * trow
            scaled.append((srow, trow))
            factors.append(later)
        b[home] = brow * lax.rsqrt(diag)
        for g in range(home + 1, groups):
            f = columns(a[g], home)
            for t in range(SUB):
                for u in range(t + 1, SUB):
                    f[u] = f[u] - f[t] * factors[t][u - t - 1]
                a[g] = a[g] - f[t] * scaled[t][0]
                b[g] = b[g] - f[t] * scaled[t][1]
    return b


def kernel(n, leading, f_ref, out_ref, a_all, f_all, gc, inv,
           own_sem, pair_send, pair_recv, ag_send, ag_recv, core_send, core_recv,
           x_send, x_recv, r_send, r_recv):
    height, width = f_ref.shape
    share = width // n
    half = height // 2
    chunks = leading // LANES
    stages = n.bit_length() - 1
    r = lax.axis_index("row")
    c = lax.axis_index("col")
    bits = [n >> (s + 1) for s in range(stages)]
    deltas = [b * (1 - 2 * (lax.rem(r // b, 2))) for b in bits]

    def ordered(parity):
        return deltas[:-2] + [
            deltas[-2] * (1 - parity) + deltas[-1] * parity,
            deltas[-1] * (1 - parity) + deltas[-2] * parity,
        ]

    def at(j, steps):
        place = r
        for s in range(stages):
            if (j >> s) & 1:
                place = place + steps[s]
        return place

    gc[...] = jnp.zeros_like(gc)
    barrier = pltpu.get_barrier_semaphore()
    for d in range(1, n):
        pl.semaphore_signal(barrier, inc=1, device_id={"row": lax.rem(r + d, n)}, device_id_type=MESH)
    pl.semaphore_signal(barrier, inc=1, device_id={"col": 1 - c}, device_id_type=MESH)
    pl.semaphore_wait(barrier, n)

    lead = f_ref.at[:, pl.ds(0, leading)]
    first = pl.ds(0, height)
    own_lead = pltpu.make_async_copy(lead, a_all.at[first, :], own_sem.at[0])
    to_pair = pltpu.make_async_remote_copy(
        src_ref=lead, dst_ref=a_all.at[first, :], send_sem=pair_send, recv_sem=pair_recv,
        device_id={"col": 1 - c}, device_id_type=MESH,
    )

    @pl.when(c == 0)
    def _():
        to_pair.start()
        own_lead.start()
        own_lead.wait()

    @pl.when(c == 1)
    def _():
        to_pair.wait_recv()

    lead_steps = ordered(c)
    quarter = 1 << (stages - 2)

    def lead_half(j):
        low = j & (quarter - 1)
        slot = low + ((j >> (stages - 2)) & 1) * quarter * (1 + c) + (j >> (stages - 1)) * quarter * (2 - c)
        return a_all.at[pl.ds(pl.multiple_of(slot * height + c * half, half), half), :]

    def lead_copy(j, s):
        k = j + (1 << s)
        return pltpu.make_async_remote_copy(
            src_ref=lead_half(j), dst_ref=lead_half(k), send_sem=ag_send.at[k], recv_sem=ag_recv.at[k],
            device_id={"row": r + lead_steps[s]}, device_id_type=MESH,
        )

    def core_copy(j):
        return pltpu.make_async_remote_copy(
            src_ref=lead_half(j), dst_ref=lead_half(j),
            send_sem=core_send.at[j], recv_sem=core_recv.at[j],
            device_id={"col": 1 - c}, device_id_type=MESH,
        )

    def share_copy(d):
        peer = at(d, deltas)
        return pltpu.make_async_remote_copy(
            src_ref=f_ref.at[:, pl.ds(pl.multiple_of(peer * share, share), share)],
            dst_ref=f_all.at[pl.ds(d * height, height), :],
            send_sem=x_send.at[d], recv_sem=x_recv.at[d],
            device_id={"row": peer}, device_id_type=MESH,
        )

    def take(j):
        top = j.bit_length() - 1
        lead_copy(j - (1 << top), top).wait_recv()
        for s in range(top + 1, stages):
            lead_copy(j, s).start()
        core_copy(j).start()

    def gram(q):
        rows = pl.ds(q * quarter * height, quarter * height)
        for k in range(chunks):
            ks = pl.ds(k * LANES, LANES)
            rest = pl.ds(k * LANES, leading - k * LANES)
            gc[ks, rest] += dot_t(a_all[rows, ks], a_all[rows, rest])

    for s in range(stages):
        lead_copy(0, s).start()
    own_share = pltpu.make_async_copy(
        f_ref.at[:, pl.ds(pl.multiple_of(r * share, share), share)], f_all.at[first, :], own_sem.at[1]
    )
    own_share.start()
    for j in range(1, 2 * quarter):
        take(j)
    for d in range(1, n):
        share_copy(d).start()
    for j in range(1, quarter):
        core_copy(j).wait_recv()
    gram(0)
    for j in range(2 * quarter, 3 * quarter):
        take(j)
    for j in range(quarter, 3 * quarter):
        core_copy(j).wait_recv()
    gram(1)
    for j in range(3 * quarter, n):
        take(j)
    gram(2)
    for j in range(3 * quarter, n):
        core_copy(j).wait_recv()
    gram(3)

    def products():
        own_share.wait()
        for d in range(1, n):
            share_copy(d).wait_recv()
        for q in range(n // quarter):
            rows = pl.ds(q * quarter * height, quarter * height)
            gc[:, pl.ds(leading, share)] += dot_t(a_all[rows, :], f_all[rows, :])

    def out_piece(k, j, steps):
        cols = pl.ds(pl.multiple_of(at(j, steps) * share, share), share)
        return out_ref.at[pl.ds(pl.multiple_of(k * LANES, LANES), LANES), cols]

    def out_copy(k, j, s):
        steps = ordered(lax.rem(k + c, 2))
        return pltpu.make_async_remote_copy(
            src_ref=out_piece(k, j, steps), dst_ref=out_piece(k, j, steps),
            send_sem=r_send.at[k, j + (1 << s)], recv_sem=r_recv.at[k, j + (1 << s)],
            device_id={"row": r + steps[s]}, device_id_type=MESH,
        )

    def forward(k, top):
        for j in range(1 << top, 2 << top):
            out_copy(k, j - (1 << top), top).wait_recv()
            for s in range(top + 1, stages):
                out_copy(k, j, s).start()

    first_col = c * width + r * share
    row_id = lax.broadcasted_iota(jnp.int32, (LANES, share), 0)
    col_id = lax.broadcasted_iota(jnp.int32, (LANES, share), 1) + first_col

    @pl.loop(0, chunks)
    def _(k):
        base = pl.multiple_of(k * LANES, LANES)
        ks = pl.ds(base, LANES)

        def read(g):
            return gc[pl.ds(pl.multiple_of(base + g * SUB, SUB), SUB), ks]

        def hook(back, top):
            def run():
                @pl.when(k >= back)
                def _():
                    forward(k - back, top)
            return run

        groups = LANES // SUB
        hooks = {2: hook(2, stages - 2)}
        for s in range(stages - 2):
            hooks[groups * (s + 1) // (stages - 1) + 1] = hook(1, s)
        b = inverse_factor(read, hooks)
        for g, part in enumerate(b):
            inv[pl.ds(g * SUB, SUB), :] = part
        pl.when(k == 0)(products)
        rows = jnp.dot(inv[...], gc[ks, :], precision=HIGHEST, preferred_element_type=jnp.float32)
        mine_out = rows[:, leading:]
        out_ref[ks, pl.ds(pl.multiple_of(r * share, share), share)] = jnp.where(
            col_id >= row_id + base, mine_out, 0.0
        )
        for s in range(stages):
            out_copy(k, 0, s).start()
        gc[ks, :] = rows
        for i in range(1, chunks):
            @pl.when(i > k)
            def _():
                left = gc[ks, pl.ds(i * LANES, LANES)]
                rest = pl.ds(i * LANES, leading + share - i * LANES)
                gc[pl.ds(i * LANES, LANES), rest] -= dot_t(left, gc[ks, rest])

    forward(chunks - 2, stages - 2)
    for top in range(stages - 1):
        forward(chunks - 1, top)
    for k in range(chunks):
        forward(k, stages - 1)

    @pl.when(c == 0)
    def _():
        to_pair.wait_send()

    for j in range(1, n):
        top = j.bit_length() - 1
        lead_copy(j - (1 << top), top).wait_send()
        core_copy(j).wait_send()
        share_copy(j).wait_send()
        for k in range(chunks):
            out_copy(k, j - (1 << top), top).wait_send()


def by_kernel(frontal, leading, n):
    height, width = frontal.shape
    share = width // n
    dma = pltpu.SemaphoreType.DMA
    return pl.pallas_call(
        functools.partial(kernel, n, leading),
        out_shape=jax.ShapeDtypeStruct((leading, width), jnp.float32),
        in_specs=[pl.BlockSpec(memory_space=pltpu.VMEM)],
        out_specs=pl.BlockSpec(memory_space=pltpu.VMEM),
        scratch_shapes=[
            pltpu.VMEM((n * height, leading), jnp.float32),
            pltpu.VMEM((n * height, share), jnp.float32),
            pltpu.VMEM((leading, leading + share), jnp.float32),
            pltpu.VMEM((LANES, LANES), jnp.float32),
            dma((2,)), dma, dma, dma((n,)), dma((n,)), dma((n,)), dma((n,)),
            dma((n,)), dma((n,)),
            dma((leading // LANES, n)), dma((leading // LANES, n)),
        ],
        compiler_params=pltpu.CompilerParams(
            collective_id=0, has_side_effects=True, vmem_limit_bytes=48 << 20
        ),
        name="front_rows",
    )(frontal)


def body(n, pair, contributions, valid_rows):
    blocks, height, width_local = contributions.shape
    live_rows = jnp.arange(height, dtype=jnp.int32)[None, :] < valid_rows[:, None]
    frontal = jnp.where(live_rows[:, :, None], contributions, 0.0).reshape(blocks * height, width_local)
    leading = NPANEL * PANEL
    rows = blocks * height
    fits = (
        pair == 2 and n >= 4 and n & (n - 1) == 0 and width_local % n == 0
        and width_local // n == LANES and rows == LANES and leading <= width_local
    )
    if fits:
        return by_kernel(frontal, leading, n)
    return by_psum(frontal, leading)


def solution(mesh):
    return jax.shard_map(
        functools.partial(body, mesh.shape["row"], mesh.shape["col"]),
        mesh=mesh,
        in_specs=(P(("front", "row"), None, "col"), P(("front", "row"))),
        out_specs=P("front", "col"),
        check_vma=False,
    )
```

profile of v0, /device:TPU:0, one launch (start us, length us, event | category | flops | bytes accessed | tf_op | source)
XLA Modules:
  0.0 101.6 jit_solution(7630559179585392700)
XLA Ops:
  0.7 1.4 %select_bitcast_fusion.f_ref = f32[128,2048]{1,0:T(8,128)S(1)} fusion(f32[1,128,2048]{2,1,0:T(8,128)} %param.2, pred[128]{0:T(512)(128)(4,1)S(1)} %iota_compare_fusion), kind=kLoop, calls=%fused_computation | loop fusion | flops 262144 | bytes 2097280 | tf_op jit(solution)/shard_map/reshape | solution.py:330
  2.0 97.6 %front_rows.1 = f32[512,2048]{1,0:T(8,128)S(1)} custom-call(f32[128,2048]{1,0:T(8,128)S(1)} %select_bitcast_fusion.f_ref), custom_call_target="tpu_custom_call" | custom-call | tf_op jit(solution)/shard_map/front_rows/pallas_call | solution.py:306
  99.6 2.0 %copy.5 = f32[512,2048]{1,0:T(8,128)} copy(f32[512,2048]{1,0:T(8,128)S(1)} %front_rows.1) | data formatting | bytes 8388608
  (1 shorter events, 0.0 us)
where the time goes:
time: 102 us
  Pallas kernels  97.6 us (96%)
  local copies, waits for them, and re-layouts  2.02 us (2%)
  other arithmetic  1.37 us (1%)
    pallas_call x1, Pallas kernels, by_kernel(): pl.pallas_call(functools.partial(kernel, n, leading), out_shape=jax.Shape...  97.6 us

commit v1 on v0

v1 whole, which is shorter than its diff:
```python
import functools

import jax
import jax.numpy as jnp
from jax import lax
from jax.experimental import pallas as pl
from jax.experimental.pallas import tpu as pltpu
from jax.sharding import PartitionSpec as P

PANEL = 256
NPANEL = 2
LANES = 128
SUB = 8
PLANE = 4
HIGHEST = lax.Precision.HIGHEST
MESH = pl.DeviceIdType.MESH


def spread(block, axis, owner):
    block = jnp.where(lax.axis_index(axis) == owner, block, jnp.zeros_like(block))
    return lax.psum(block, axis)


def inner_cols(left, right):
    return jnp.einsum("rp,rc->pc", left, right, precision=HIGHEST)


def by_psum(frontal, leading):
    width_local = frontal.shape[1]
    leading_cols = spread(frontal[:, :leading], "col", 0)
    gram_total = lax.psum(inner_cols(leading_cols, leading_cols), "row")
    factor = jnp.linalg.cholesky(gram_total)
    identity = jnp.eye(leading, dtype=jnp.float32)
    inverse = jax.scipy.linalg.solve_triangular(factor, identity, lower=True)
    first_basis = jnp.dot(leading_cols, inverse.T, precision=HIGHEST)
    projected = lax.psum(inner_cols(first_basis, frontal), "row")
    column_ids = lax.axis_index("col") * width_local + jnp.arange(width_local, dtype=jnp.int32)
    kept_mask = column_ids[None, :] >= jnp.arange(leading, dtype=jnp.int32)[:, None]
    return jnp.where(kept_mask, projected, jnp.zeros_like(projected))


def dot_t(left, right):
    return lax.dot_general(
        left, right, (((0,), (0,)), ((), ())), precision=HIGHEST, preferred_element_type=jnp.float32
    )


def inverse_factor(read, hooks):
    groups = LANES // SUB
    tile = (SUB, LANES)
    row = lax.broadcasted_iota(jnp.int32, tile, 0)
    col = lax.broadcasted_iota(jnp.int32, tile, 1)
    a = [read(g) for g in range(groups)]
    b = [jnp.where(row + g * SUB == col, 1.0, 0.0).astype(jnp.float32) for g in range(groups)]

    def columns(value, home):
        first = home * SUB
        return [jnp.broadcast_to(value[:, first + t : first + t + 1], tile) for t in range(SUB)]

    def across(value, t):
        return jnp.broadcast_to(value[t : t + 1, :], tile)

    for home in range(groups):
        if home in hooks:
            hooks[home]()
        f = columns(a[home], home)
        arow, brow = a[home], b[home]
        scaled, factors = [], []
        diag = f[0]
        for t in range(SUB):
            pinv = 1.0 / across(f[t], t)
            diag = jnp.where(row == t, f[t], diag)
            srow = across(arow, t) * pinv
            trow = across(brow, t) * pinv
            later = [across(f[u], t) * pinv for u in range(t + 1, SUB)]
            below = jnp.where(row > t, f[t], 0.0)
            for u in range(t + 1, SUB):
                f[u] = f[u] - below * later[u - t - 1]
            if t < SUB - 1:
                arow = arow - below * srow
                brow = brow - below * trow
            scaled.append((srow, trow))
            factors.append(later)
        b[home] = brow * lax.rsqrt(diag)
        for g in range(home + 1, groups):
            f = columns(a[g], home)
            for t in range(SUB):
                for u in range(t + 1, SUB):
                    f[u] = f[u] - f[t] * factors[t][u - t - 1]
                a[g] = a[g] - f[t] * scaled[t][0]
                b[g] = b[g] - f[t] * scaled[t][1]
    return b


def kernel(n, leading, f_ref, out_ref, a_pl, f_pl, gram, gram_in, gram_out, part, part_in, gc, inv,
           own_sem, pair_send, pair_recv, ag_send, ag_recv, core_send, core_recv, f_send, f_recv,
           gz_send, gz_recv, gp_send, gp_recv, p_send, p_recv, r_send, r_recv):
    height, width = f_ref.shape
    share = width // n
    half = height // 2
    chunks = leading // LANES
    planes = n // PLANE
    span = planes * share
    slab = LANES // (2 * PLANE)
    stages = n.bit_length() - 1
    r = lax.axis_index("row")
    c = lax.axis_index("col")
    q = lax.rem(r, PLANE)
    z = r // PLANE
    mine = (2 * q + c) * slab
    deltas = [(1 << s) * (1 - 2 * lax.rem(r // (1 << s), 2)) for s in range(stages)]

    def beside(d):
        place = r
        for s in range(stages):
            if (d >> s) & 1:
                place = place + deltas[s]
        return place

    def column(place):
        return pl.multiple_of((lax.rem(place, PLANE) * planes + place // PLANE) * share, share)

    in_plane = list(range(1, PLANE))
    in_line = [PLANE * d for d in range(1, planes)]

    gc[...] = jnp.zeros_like(gc)
    barrier = pltpu.get_barrier_semaphore()
    for d in in_plane + in_line:
        pl.semaphore_signal(barrier, inc=1, device_id={"row": beside(d)}, device_id_type=MESH)
    pl.semaphore_signal(barrier, inc=1, device_id={"col": 1 - c}, device_id_type=MESH)
    pl.semaphore_wait(barrier, len(in_plane) + len(in_line) + 1)

    def to(place):
        return {"device_id": {"row": place}, "device_id_type": MESH}

    other = {"device_id": {"col": 1 - c}, "device_id_type": MESH}
    lead_cols = pl.ds(0, leading)
    lead_steps = [deltas[0] * (1 - c) + deltas[1] * c, deltas[1] * (1 - c) + deltas[0] * c]

    def to_pair(h):
        rows = pl.ds(h * half, half)
        return pltpu.make_async_remote_copy(
            src_ref=f_ref.at[rows, lead_cols], dst_ref=a_pl.at[rows, :],
            send_sem=pair_send.at[h], recv_sem=pair_recv.at[h], **other,
        )

    def lead_half(j):
        slot = (j & 1) * (1 + c) + (j >> 1) * (2 - c)
        return a_pl.at[pl.ds(pl.multiple_of(slot * height + c * half, half), half), :]

    def lead_copy(j, s, src=None):
        k = j + (1 << s)
        return pltpu.make_async_remote_copy(
            src_ref=lead_half(j) if src is None else src, dst_ref=lead_half(k),
            send_sem=ag_send.at[k], recv_sem=ag_recv.at[k], **to(r + lead_steps[s]),
        )

    def core_copy(j):
        return pltpu.make_async_remote_copy(
            src_ref=lead_half(j), dst_ref=lead_half(j),
            send_sem=core_send.at[j], recv_sem=core_recv.at[j], **other,
        )

    own_lead = pltpu.make_async_copy(f_ref.at[:, lead_cols], a_pl.at[pl.ds(0, height), :], own_sem.at[0])
    own_f = pltpu.make_async_copy(
        f_ref.at[:, pl.ds(pl.multiple_of(q * span, span), span)], f_pl.at[pl.ds(0, height), :], own_sem.at[1]
    )

    def f_copy(d):
        place = beside(d)
        return pltpu.make_async_remote_copy(
            src_ref=f_ref.at[:, pl.ds(pl.multiple_of(lax.rem(place, PLANE) * span, span), span)],
            dst_ref=f_pl.at[pl.ds(d * height, height), :],
            send_sem=f_send.at[d], recv_sem=f_recv.at[d], **to(place),
        )

    def tail(k):
        return pl.ds(k * LANES, leading - k * LANES)

    def slab_of(k):
        return pl.ds(pl.multiple_of(k * LANES + mine, slab), slab)

    def gram_line(k, d):
        return pltpu.make_async_remote_copy(
            src_ref=gram.at[slab_of(k), tail(k)], dst_ref=gram_in.at[z, pl.ds(k * slab, slab), tail(k)],
            send_sem=gz_send.at[k, d // PLANE], recv_sem=gz_recv.at[k, d // PLANE], **to(beside(d)),
        )

    def gram_plane(k, i):
        return pltpu.make_async_remote_copy(
            src_ref=gram_out.at[pl.ds(k * slab, slab), tail(k)], dst_ref=gc.at[slab_of(k), tail(k)],
            send_sem=gp_send.at[k, i], recv_sem=gp_recv.at[k, i],
            device_id={"row": beside(i // 2), "col": c + (i % 2) * (1 - 2 * c)}, device_id_type=MESH,
        )

    others = range(1, 2 * PLANE)

    def gram_sum(k):
        for d in in_line:
            gram_line(k, d).wait_recv()
        rows = pl.ds(k * slab, slab)
        gram_in[z, rows, tail(k)] = gram[slab_of(k), tail(k)]
        total = gram_in[0, rows, tail(k)]
        for p in range(1, planes):
            total = total + gram_in[p, rows, tail(k)]
        gram_out[rows, tail(k)] = total
        gc[slab_of(k), tail(k)] = total
        for i in others:
            gram_plane(k, i).start()

    def chunk_rows(k):
        return pl.ds(pl.multiple_of(k * LANES, LANES), LANES)

    def part_copy(k, d):
        place = beside(d)
        return pltpu.make_async_remote_copy(
            src_ref=part.at[chunk_rows(k), pl.ds(pl.multiple_of(place // PLANE * share, share), share)],
            dst_ref=part_in.at[d // PLANE - 1, chunk_rows(k), :],
            send_sem=p_send.at[k, d // PLANE], recv_sem=p_recv.at[k, d // PLANE], **to(place),
        )

    def product(k):
        part[chunk_rows(k), :] = dot_t(a_pl[:, chunk_rows(k)], f_pl[...])
        for d in in_line:
            part_copy(k, d).start()

    def add_product(k):
        for d in in_line:
            part_copy(k, d).wait_recv()
        rows = chunk_rows(k)
        total = part[rows, pl.ds(pl.multiple_of(z * share, share), share)]
        for i in range(planes - 1):
            total = total + part_in[i, rows, :]
        gc[rows, pl.ds(leading, share)] += total

    @pl.when(c == 0)
    def _():
        to_pair(1).start()
        for s in range(2):
            lead_copy(0, s, f_ref.at[pl.ds(0, half), lead_cols]).start()
        to_pair(0).start()
        own_lead.start()

    @pl.when(c == 1)
    def _():
        to_pair(1).wait_recv()
        for s in range(2):
            lead_copy(0, s).start()

    own_f.start()
    lead_copy(0, 0).wait_recv()
    lead_copy(1, 1).start()
    core_copy(1).start()
    lead_copy(0, 1).wait_recv()
    core_copy(2).start()
    for d in reversed(in_plane):
        f_copy(d).start()
    lead_copy(1, 1).wait_recv()
    core_copy(3).start()

    @pl.when(c == 0)
    def _():
        own_lead.wait()

    @pl.when(c == 1)
    def _():
        to_pair(0).wait_recv()

    for j in in_plane:
        core_copy(j).wait_recv()
    for k in range(chunks):
        rows = pl.ds(k * LANES, LANES)
        gram[rows, tail(k)] = dot_t(a_pl[:, rows], a_pl[:, tail(k)])
        for d in in_line:
            gram_line(k, d).start()
    gram_sum(0)
    own_f.wait()
    for d in in_plane:
        f_copy(d).wait_recv()
    product(0)
    for k in range(1, chunks):
        gram_sum(k)
    product(1)
    for i in others:
        gram_plane(0, i).wait_recv()

    def steps_of(parity):
        return [
            deltas[3], deltas[2],
            deltas[1] * (1 - parity) + deltas[0] * parity,
            deltas[0] * (1 - parity) + deltas[1] * parity,
        ]

    def out_piece(k, j, steps):
        place = r
        for s in range(stages):
            if (j >> s) & 1:
                place = place + steps[s]
        return out_ref.at[chunk_rows(k), pl.ds(column(place), share)]

    def out_copy(k, j, s):
        steps = steps_of(lax.rem(k + c, 2))
        return pltpu.make_async_remote_copy(
            src_ref=out_piece(k, j, steps), dst_ref=out_piece(k, j, steps),
            send_sem=r_send.at[k, j + (1 << s)], recv_sem=r_recv.at[k, j + (1 << s)], **to(r + steps[s]),
        )

    def forward(k, top):
        for j in range(1 << top, 2 << top):
            out_copy(k, j - (1 << top), top).wait_recv()
            for s in range(top + 1, stages):
                out_copy(k, j, s).start()

    first_col = c * width + column(r)
    row_id = lax.broadcasted_iota(jnp.int32, (LANES, share), 0)
    col_id = lax.broadcasted_iota(jnp.int32, (LANES, share), 1) + first_col

    @pl.loop(0, chunks)
    def _(k):
        base = pl.multiple_of(k * LANES, LANES)
        ks = pl.ds(base, LANES)

        def read(g):
            return gc[pl.ds(pl.multiple_of(base + g * SUB, SUB), SUB), ks]

        def hook(back, top):
            def run():
                @pl.when(k >= back)
                def _():
                    forward(k - back, top)
            return run

        groups = LANES // SUB
        hooks = {2: hook(2, stages - 2)}
        for s in range(stages - 2):
            hooks[groups * (s + 1) // (stages - 1) + 1] = hook(1, s)
        b = inverse_factor(read, hooks)
        for g, rows in enumerate(b):
            inv[pl.ds(g * SUB, SUB), :] = rows
        add_product(k)
        rows = jnp.dot(inv[...], gc[ks, :], precision=HIGHEST, preferred_element_type=jnp.float32)
        out_ref[ks, pl.ds(column(r), share)] = jnp.where(col_id >= row_id + base, rows[:, leading:], 0.0)
        for s in range(stages):
            out_copy(k, 0, s).start()
        gc[ks, :] = rows

        @pl.when(k == 0)
        def _():
            for g in range(1, chunks):
                for i in others:
                    gram_plane(g, i).wait_recv()

        for i in range(1, chunks):
            @pl.when(i > k)
            def _():
                left = gc[ks, pl.ds(i * LANES, LANES)]
                rest = pl.ds(i * LANES, leading + share - i * LANES)
                gc[pl.ds(i * LANES, LANES), rest] -= dot_t(left, gc[ks, rest])

        @pl.when(k + 2 < chunks)
        def _():
            product(k + 2)

    forward(chunks - 2, stages - 2)
    for top in range(stages - 1):
        forward(chunks - 1, top)
    for k in range(chunks):
        forward(k, stages - 1)

    @pl.when(c == 0)
    def _():
        for h in range(2):
            to_pair(h).wait_send()

    for d in in_plane:
        lead_copy(0 if d < 3 else 1, 0 if d == 1 else 1).wait_send()
        core_copy(d).wait_send()
        f_copy(d).wait_send()
    for k in range(chunks):
        for d in in_line:
            gram_line(k, d).wait_send()
            part_copy(k, d).wait_send()
        for i in others:
            gram_plane(k, i).wait_send()
        for j in range(1, n):
            top = j.bit_length() - 1
            out_copy(k, j - (1 << top), top).wait_send()


def by_kernel(frontal, leading, n):
    height, width = frontal.shape
    share = width // n
    chunks = leading // LANES
    planes = n // PLANE
    slab = LANES // (2 * PLANE)
    dma = pltpu.SemaphoreType.DMA
    return pl.pallas_call(
        functools.partial(kernel, n, leading),
        out_shape=jax.ShapeDtypeStruct((leading, width), jnp.float32),
        in_specs=[pl.BlockSpec(memory_space=pltpu.VMEM)],
        out_specs=pl.BlockSpec(memory_space=pltpu.VMEM),
        scratch_shapes=[
            pltpu.VMEM((PLANE * height, leading), jnp.float32),
            pltpu.VMEM((PLANE * height, planes * share), jnp.float32),
            pltpu.VMEM((leading, leading), jnp.float32),
            pltpu.VMEM((planes, chunks * slab, leading), jnp.float32),
            pltpu.VMEM((chunks * slab, leading), jnp.float32),
            pltpu.VMEM((leading, planes * share), jnp.float32),
            pltpu.VMEM((planes - 1, leading, share), jnp.float32),
            pltpu.VMEM((leading, leading + share), jnp.float32),
            pltpu.VMEM((LANES, LANES), jnp.float32),
            dma((2,)), dma((2,)), dma((2,)), dma((PLANE,)), dma((PLANE,)), dma((PLANE,)), dma((PLANE,)),
            dma((PLANE,)), dma((PLANE,)),
            dma((chunks, planes)), dma((chunks, planes)),
            dma((chunks, 2 * PLANE)), dma((chunks, 2 * PLANE)),
            dma((chunks, planes)), dma((chunks, planes)),
            dma((chunks, n)), dma((chunks, n)),
        ],
        compiler_params=pltpu.CompilerParams(
            collective_id=0, has_side_effects=True, vmem_limit_bytes=48 << 20
        ),
        name="front_rows",
    )(frontal)


def body(n, pair, contributions, valid_rows):
    blocks, height, width_local = contributions.shape
    live_rows = jnp.arange(height, dtype=jnp.int32)[None, :] < valid_rows[:, None]
    frontal = jnp.where(live_rows[:, :, None], contributions, 0.0).reshape(blocks * height, width_local)
    leading = NPANEL * PANEL
    rows = blocks * height
    fits = (
        pair == 2 and n == PLANE * PLANE and width_local == n * LANES
        and rows == LANES and leading % LANES == 0 and leading <= width_local
    )
    if fits:
        return by_kernel(frontal, leading, n)
    return by_psum(frontal, leading)


def solution(mesh):
    return jax.shard_map(
        functools.partial(body, mesh.shape["row"], mesh.shape["col"]),
        mesh=mesh,
        in_specs=(P(("front", "row"), None, "col"), P(("front", "row"))),
        out_specs=P("front", "col"),
        check_vma=False,
    )
```

time: 102 us -> 96 us (0.941)
  Pallas kernels: 97.6 us -> 91.8 us
    pallas_call x1, Pallas kernels: 97.6 us -> 91.8 us  [by_kernel(): pl.pallas_call(functools.partial(kernel, n, leading), out_shape=jax.Shape...]
where the time goes in v1:
time: 96 us; the launch traced here: 95.9 us
  Pallas kernels  91.8 us (96%)
  local copies, waits for them, and re-layouts  2.02 us (2%)
  other arithmetic  1.37 us (1%)
    pallas_call x1, Pallas kernels, by_kernel(): pl.pallas_call(functools.partial(kernel, n, leading), out_shape=jax.Shape...  91.8 us
    unnamed x1, local copies, waits for them, and re-layouts  2.02 us

profile of v1, /device:TPU:0, one launch (start us, length us, event | category | flops | bytes accessed | tf_op | source)
XLA Modules:
  0.0 95.9 jit_solution(16847032310993396424)
XLA Ops:
  0.7 1.4 %select_bitcast_fusion.f_ref = f32[128,2048]{1,0:T(8,128)S(1)} fusion(f32[1,128,2048]{2,1,0:T(8,128)} %param.2, pred[128]{0:T(512)(128)(4,1)S(1)} %iota_compare_fusion), kind=kLoop, calls=%fused_computation | loop fusion | flops 262144 | bytes 2097280 | tf_op jit(solution)/shard_map/reshape | solution.py:429
  2.0 91.8 %front_rows.1 = f32[512,2048]{1,0:T(8,128)S(1)} custom-call(f32[128,2048]{1,0:T(8,128)S(1)} %select_bitcast_fusion.f_ref), custom_call_target="tpu_custom_call" | custom-call | tf_op jit(solution)/shard_map/front_rows/pallas_call | solution.py:397
  93.8 2.0 %copy.5 = f32[512,2048]{1,0:T(8,128)} copy(f32[512,2048]{1,0:T(8,128)S(1)} %front_rows.1) | data formatting | bytes 8388608
  (1 shorter events, 0.0 us)
